TPU v7x, 256 devices: a whole 4x4x8 slice. The times are simulated.
256 devices in a mesh: row: 2 (over core), col: 64 (over z, y, x_hi), layer: 2 (over x_lo).
Axes of the slice: x: 4 (x_hi: 2, x_lo: 2; x = x_hi * 2 + x_lo), y: 4, z: 8, core: 2. Of those that a mesh axis runs over, the one named last changes fastest.
Arguments:
- flow_cols: int32 [16, 2, 64], P('row', 'layer', 'col'), may hold values from 0 to 64, as said below
- flow_vals: bfloat16 [16, 2, 64, 128, 128], P('row', 'layer', 'col'), may hold values from -22 to 22
- window_flow: bfloat16 [2, 8192, 32768], P('layer', 'row', 'col'), may hold values from -0.1403165 to 0.1403165
Outputs:
- flow_next: float32 [2048, 32768], P(('row', 'layer'), 'col')
Inputs may be any that keep to these rules, and one draw needn't show every extreme that they name: `flow_cols`: an entry 64 marks an empty slot; the live entries of one block row and layer are distinct; every block row and layer has at least one live slot, and some block row and layer has all 64 slots live.
All inputs are finite; a program needn't handle non-finite values.
Results may differ from a plain program's by a relative error of at most 0.0003.
Values may be sent and summed in bfloat16 or wider, within the bound.
A program may use at most 128 MiB of HBM per device.

v0:
```python
import jax
import jax.numpy as jnp
from jax import lax
from jax.sharding import PartitionSpec as P


def body(flow_cols, flow_vals, window_flow):
    window_panel = lax.all_gather(window_flow[0], "row", axis=0, tiled=True)
    block_size = flow_vals.shape[-1]
    block_count = window_panel.shape[0] // block_size
    row_blocks = flow_vals.shape[0]
    all_cols, all_vals = (
        lax.all_gather(flow_cols, "col", axis=2, tiled=True),
        lax.all_gather(flow_vals, "col", axis=2, tiled=True),
    )
    slot_cols = all_cols[:, 0, :]
    slot_vals = all_vals[:, 0]
    column_ids = jnp.arange(block_count, dtype=jnp.int32)
    one_hot = (slot_cols[:, :, None] == column_ids[None, None, :]).astype(jnp.bfloat16)
    dense_row = jnp.einsum(
        "isab,isk->iakb", slot_vals, one_hot, preferred_element_type=jnp.bfloat16
    )
    dense_row = dense_row.reshape(row_blocks * block_size, block_count * block_size)
    expanded = jnp.dot(dense_row, window_panel, preferred_element_type=jnp.float32)
    total_rows = row_blocks * block_size * lax.axis_size("row")
    summed = lax.psum(expanded, "layer")
    all_squares = summed * summed
    column_sums = lax.psum(jnp.sum(all_squares, axis=0), "row")
    share_rows = summed.shape[0] // lax.axis_size("layer")
    squares = lax.dynamic_slice_in_dim(
        all_squares, lax.axis_index("layer") * share_rows, share_rows, 0
    )
    return squares / (column_sums / total_rows + 1e-06)


def solution(mesh):
    placed = (
        P("row", "layer", "col"),
        P("row", "layer", "col", None, None),
        P("layer", "row", "col"),
    )
    return jax.shard_map(
        body, mesh=mesh, in_specs=placed, out_specs=P(("row", "layer"), "col"), check_vma=False
    )
```

profile of v0, /device:TPU:1, one launch (start us, length us, event | category | flops | bytes accessed | tf_op | source)
XLA Modules:
  0.0 361.2 jit_solution(3582234207168179350)
XLA Ops:
  6.5 0.0 all-gather.4.cloned.1.call-start
  6.5 0.7 all-gather.4.cloned.1.call-update
  7.3 0.0 all-gather.6.cloned.1.call-start
  7.3 0.7 all-gather.6.cloned.1.call-update
  8.0 0.0 all-reduce.2.cloned.1.call-start
  8.1 156.8 %all_gather.9 = s32[8,1,64]{0,1,2:T(1,128)S(1)} all-gather(s32[8,1,1]{0,1,2:T(1,128)} %bitcast.23), channel_id=1, replica_groups=mesh['row'=2,'col'=64,'layer'=2] {'col'}, dimensions={2}, use_global_device_ids=true | all-gather | bytes 2080 | tf_op jit(solution)/shard_map/all_gather | solution.py:13
  164.9 0.1 copy.7
  165.0 58.9 %all-gather.4.cloned.1.call-done = bf16[8,1,64,128,128]{4,3,1,0,2:T(8,128)(2,1)} async-done(((bf16[8,1,1,128,128]{4,3,1,0,2:T(8,128)(2,1)}), bf16[8,1,64,128,128]{4,3,1,0,2:T(8,128)(2,1)}) %all-gather.4.cloned.1.call-update) | async-done | bytes 16777232 | tf_op jit(solution)/shard_map/all_gather | solution.py:14
  223.9 22.9 %fusion.3 = bf16[8,64,128,128]{3,1,2,0:T(8,128)(2,1)} fusion(bf16[8,1,64,128,128]{4,3,1,0,2:T(8,128)(2,1)} %all-gather.4.cloned.1.call-done, s32[8,64]{1,0:T(8,128)S(1)} %copy.7), kind=kOutput, calls=%fused_computation.3 | convolution fusion | flops 1073774592 | bytes 33556480 | tf_op jit(solution)/shard_map/isab,isk->iakb/dot_general | solution.py:20
  246.8 2.1 all-gather.6.cloned.1.call-done
  248.9 24.6 %fusion = f32[1024,512]{1,0:T(8,128)} fusion(bf16[128,8,64,128]{3,2,1,0:T(8,128)(2,1)} %bitcast.20, bf16[1,8192,512]{2,1,0:T(8,128)(2,1)} %all-gather.6.cloned.1.call-done), kind=kOutput, calls=%fused_computation | convolution fusion | flops 8589934592 | bytes 27262976 | tf_op jit(solution)/shard_map/dot_general | solution.py:24
  273.5 0.0 all-reduce.2.cloned.1.call-update
  273.5 75.3 %all-reduce.2.cloned.1.call-done = f32[1024,512]{1,0:T(8,128)} async-done(((f32[1024,512]{1,0:T(8,128)}), f32[1024,512]{1,0:T(8,128)}) %all-reduce.2.cloned.1.call-update) | async-done | bytes 2097168 | tf_op jit(solution)/shard_map/psum | solution.py:26
  348.8 1.9 multiply_reduce_fusion
  350.7 2.8 psum.15
  353.6 1.1 dynamic-slice_divide_fusion
  (1 shorter events, 0.0 us)
Async XLA Ops:
  6.5 217.4 %all-gather.4.cloned.1.call-start = ((), (), s32[]{:S(2)}) async-start(), calls=%async_computation | async-start | bytes 17039360 | tf_op jit(solution)/shard_map/all_gather | solution.py:14
  7.3 241.6 %all-gather.6.cloned.1.call-start = ((), (), s32[]{:S(2)}) async-start(), calls=%async_computation.2 | async-start | bytes 12582912 | tf_op jit(solution)/shard_map/all_gather | solution.py:8
  8.0 340.8 %all-reduce.2.cloned.1.call-start = ((), (), s32[]{:S(2)}) async-start(), calls=%async_computation.1 | async-start | bytes 4194304 | tf_op jit(solution)/shard_map/psum | solution.py:26
Sparse Core Ops, SparseCore 0:
  11.1 212.7 all-gather.3
  225.7 23.1 all-gather.5
  273.6 75.1 all-reduce.1
where the time goes:
time: 361 us
  blocking collectives  160 us (44%)
  waiting for transfers between devices  138 us (38%)
  matrix products  47.5 us (13%)
  between operations  13.1 us (4%)
    all_gather x1, blocking collectives, body(): lax.all_gather(flow_cols, 'col', axis=2, tiled=True)  157 us
    psum x1, waiting for transfers between devices, body(): summed = lax.psum(expanded, 'layer')  75.3 us
    all_gather x1, waiting for transfers between devices, body(): lax.all_gather(flow_vals, 'col', axis=2, tiled=True)  58.9 us
    dot_general x1, matrix products, body(): jnp.dot(dense_row, window_panel, preferred_element_type=jnp.float32)  24.6 us
    dot_general x1, matrix products, body(): jnp.einsum('isab,isk->iakb', slot_vals, one_hot, preferred_element_type=j...  22.9 us
  transfers between devices with their start and end apart: 3, of which 3 were waited for; matrix products, arithmetic and copies ran while one was open for 6% of the time, Pallas kernels for 0%

commit v1 on v0

--- a/solution.py
+++ b/solution.py
@@ -23,7 +23,8 @@
     dense_row = dense_row.reshape(row_blocks * block_size, block_count * block_size)
     expanded = jnp.dot(dense_row, window_panel, preferred_element_type=jnp.float32)
     total_rows = row_blocks * block_size * lax.axis_size("row")
-    summed = lax.psum(expanded, "layer")
+    parts = lax.all_gather(expanded, "layer", axis=0, tiled=False)
+    summed = parts.sum(axis=0)
     all_squares = summed * summed
     column_sums = lax.psum(jnp.sum(all_squares, axis=0), "row")
     share_rows = summed.shape[0] // lax.axis_size("layer")

time: 361 us -> 352 us (0.975)
  waiting for transfers between devices: 138 us -> 125 us
  other arithmetic: 2.99 us -> 6.78 us
    psum x1 -> x0, waiting for transfers between devices: 75.3 us -> none  [body(): summed = lax.psum(expanded, 'layer')]
    all_gather x0 -> x1, waiting for transfers between devices: none -> 62.5 us  [body(): parts = lax.all_gather(expanded, 'layer', axis=0, tiled=False)]
  transfers between devices with their start and end apart: 3 -> 3, of which waited for: 3 -> 3; matrix products, arithmetic and copies ran while one was open for 6% -> 7% of each run, Pallas kernels for 0% -> 0%
where the time goes in v1:
time: 352 us
  blocking collectives  160 us (45%)
  waiting for transfers between devices  125 us (36%)
  matrix products  47.5 us (13%)
  between operations  13.1 us (4%)
  other arithmetic  6.78 us (2%)
    all_gather x1, blocking collectives, body(): lax.all_gather(flow_cols, 'col', axis=2, tiled=True)  157 us
    all_gather x1, waiting for transfers between devices, body(): parts = lax.all_gather(expanded, 'layer', axis=0, tiled=False)  62.5 us
    all_gather x1, waiting for transfers between devices, body(): lax.all_gather(flow_vals, 'col', axis=2, tiled=True)  58.9 us
    dot_general x1, matrix products, body(): jnp.dot(dense_row, window_panel, preferred_element_type=jnp.float32)  24.6 us
    dot_general x1, matrix products, body(): jnp.einsum('isab,isk->iakb', slot_vals, one_hot, preferred_element_type=j...  22.9 us
  transfers between devices with their start and end apart: 3, of which 3 were waited for; matrix products, arithmetic and copies ran while one was open for 7% of the time, Pallas kernels for 0%

profile of v1, /device:TPU:1, one launch (start us, length us, event | category | flops | bytes accessed | tf_op | source)
XLA Modules:
  0.0 352.1 jit_solution(15074289938609419050)
XLA Ops:
  6.5 0.0 all-gather.6.cloned.1.call-start
  6.5 0.7 all-gather.6.cloned.1.call-update
  7.3 0.0 all-gather.8.cloned.1.call-start
  7.3 0.7 all-gather.8.cloned.1.call-update
  8.0 0.0 all-gather.10.cloned.1.call-start
  8.1 156.8 %all_gather.15 = s32[8,1,64]{0,1,2:T(1,128)S(1)} all-gather(s32[8,1,1]{0,1,2:T(1,128)} %bitcast.25), channel_id=1, replica_groups=mesh['row'=2,'col'=64,'layer'=2] {'col'}, dimensions={2}, use_global_device_ids=true | all-gather | bytes 2080 | tf_op jit(solution)/shard_map/all_gather | solution.py:13
  164.9 0.1 copy.7
  165.0 58.9 %all-gather.6.cloned.1.call-done = bf16[8,1,64,128,128]{4,3,1,0,2:T(8,128)(2,1)} async-done(((bf16[8,1,1,128,128]{4,3,1,0,2:T(8,128)(2,1)}), bf16[8,1,64,128,128]{4,3,1,0,2:T(8,128)(2,1)}) %all-gather.6.cloned.1.call-update) | async-done | bytes 16777232 | tf_op jit(solution)/shard_map/all_gather | solution.py:14
  223.9 22.9 %fusion.3 = bf16[8,64,128,128]{3,1,2,0:T(8,128)(2,1)} fusion(bf16[8,1,64,128,128]{4,3,1,0,2:T(8,128)(2,1)} %all-gather.6.cloned.1.call-done, s32[8,64]{1,0:T(8,128)S(1)} %copy.7), kind=kOutput, calls=%fused_computation.3 | convolution fusion | flops 1073774592 | bytes 33556480 | tf_op jit(solution)/shard_map/isab,isk->iakb/dot_general | solution.py:20
  246.8 2.1 all-gather.8.cloned.1.call-done
  248.9 24.6 %fusion = f32[1024,512]{1,0:T(8,128)} fusion(bf16[128,8,64,128]{3,2,1,0:T(8,128)(2,1)} %bitcast.21, bf16[1,8192,512]{2,1,0:T(8,128)(2,1)} %all-gather.8.cloned.1.call-done), kind=kOutput, calls=%fused_computation | convolution fusion | flops 8589934592 | bytes 27262976 | tf_op jit(solution)/shard_map/dot_general | solution.py:24
  273.5 0.0 all-gather.10.cloned.1.call-update
  273.5 62.5 %all-gather.10.cloned.1.call-done = f32[2048,512]{1,0:T(8,128)} async-done(((f32[1024,512]{1,0:T(8,128)}), f32[2048,512]{1,0:T(8,128)}) %all-gather.10.cloned.1.call-update) | async-done | bytes 4194320 | tf_op jit(solution)/shard_map/all_gather | solution.py:26
  336.0 2.9 reduce_sum.18
  338.9 1.6 multiply_reduce_fusion
  340.5 2.8 psum.7
  343.2 2.3 dynamic-slice_divide_fusion
  (1 shorter events, 0.0 us)
Async XLA Ops:
  6.5 217.4 %all-gather.6.cloned.1.call-start = ((), (), s32[]{:S(2)}) async-start(), calls=%async_computation | async-start | bytes 17039360 | tf_op jit(solution)/shard_map/all_gather | solution.py:14
  7.3 241.6 %all-gather.8.cloned.1.call-start = ((), (), s32[]{:S(2)}) async-start(), calls=%async_computation.1 | async-start | bytes 12582912 | tf_op jit(solution)/shard_map/all_gather | solution.py:8
  8.0 328.0 %all-gather.10.cloned.1.call-start = ((), (), s32[]{:S(2)}) async-start(), calls=%async_computation.2 | async-start | bytes 6291456 | tf_op jit(solution)/shard_map/all_gather | solution.py:26
Sparse Core Ops, SparseCore 0:
  11.1 212.7 all-gather.5
  225.7 23.1 all-gather.7
  273.6 62.3 all-gather.9
